TPU v7x, 32 devices: a whole 2x2x4 slice. The times are simulated.
32 devices in a mesh: dom: 16 (over z, x, core), mem: 2 (over y).
Axes of the slice: x: 2, y: 2, z: 4, core: 2. Of those that a mesh axis runs over, the one named last changes fastest.
Arguments:
- ensemble: bfloat16 [12, 32, 65536], P('mem', None, 'dom'), may hold values from -6 to 6
- observed: float32 [32, 16384], P(None, 'dom'), may hold values from -6 to 6
- tile_weight: bfloat16 [1536, 128, 128], P('dom')
- tile_block: int32 [1536], P('dom'), may hold values from 0 to 31
- tile_target: int32 [1536], P('dom'), may hold values from 0 to 127, as said below
- tile_count: int32 [16], P('dom'), may hold values from 48 to 96, as said below
Outputs:
- crps: float32 [32, 16384], P(None, 'dom')
Inputs may be any that keep to these rules, and one draw needn't show every extreme that they name: `tile_block`: a slot's source block, counted within its partition's cells. `tile_target`: slot k belongs to partition p = k // 96; its target tile is owned by one of the partitions p - 4 to p + 4, where partition o owns the 8 target tiles from o * 8 on. The live slots of partition p are the first tile_count[p] of its list; the rest are padding.
All inputs are finite; a program needn't handle non-finite values.
Results may differ from a plain program's by a relative error of at most 0.0003.
Values sent between devices are 32-bit elements; how exact they have to be, the bound alone decides.
A program may use at most 64 MiB of HBM per device.

v0:
```python
import math
import jax
import jax.numpy as jnp
from jax import lax
from jax.sharding import PartitionSpec as P

REACH = 4


def from_behind(value, axis, steps):
    count = lax.axis_size(axis)
    first, last = (max(0, -steps), min(count, count - steps))
    return lax.ppermute(value, axis, [(source, source + steps) for source in range(first, last)])


def pair_total(left_set, right_set):
    flat_left = left_set.reshape(left_set.shape[0], -1)
    flat_right = right_set.reshape(right_set.shape[0], -1)
    total_columns = flat_left.shape[1]
    block_span = math.gcd(total_columns, 1024)

    def block_pairs(first_column):
        left_cols = lax.dynamic_slice_in_dim(flat_left, first_column, block_span, 1)
        right_cols = lax.dynamic_slice_in_dim(flat_right, first_column, block_span, 1)
        return jnp.sum(jnp.abs(left_cols[:, None, :] - right_cols[None, :, :]), axis=(0, 1))

    column_starts = jnp.arange(total_columns // block_span, dtype=jnp.int32) * block_span
    return lax.map(block_pairs, column_starts).reshape(left_set.shape[1:])


def on_device(ensemble, observed, tile_weight, tile_block, tile_target, tile_count):
    groups, levels, src_cells = ensemble.shape
    block_cells = tile_weight.shape[1]
    channels = groups * levels
    tile_slots = tile_block.shape[0]
    values = ensemble.reshape(channels, src_cells // block_cells, block_cells)
    picked = jnp.take(values, tile_block, axis=1)
    partial_value = jnp.einsum(
        "csi,sij->scj", picked, tile_weight, preferred_element_type=jnp.float32
    )
    owned = observed.shape[1] // block_cells
    window = 2 * REACH + 1
    device = lax.axis_index("dom")
    local_tile = tile_target - (device - REACH) * owned
    rows_index = jnp.arange(window * owned, dtype=jnp.int32)
    is_live = jnp.arange(tile_slots, dtype=jnp.int32) < tile_count[0]
    chooser = ((rows_index[:, None] == local_tile[None, :]) & is_live[None, :]).astype(jnp.float32)
    owner_parts = jnp.dot(
        chooser,
        partial_value.reshape(tile_slots, channels * block_cells),
        precision=lax.Precision.HIGHEST,
        preferred_element_type=jnp.float32,
    )
    owner_parts = owner_parts.reshape(window, owned, channels * block_cells)
    summed = owner_parts[REACH]
    for offset in range(-REACH, REACH + 1):
        if offset != 0:
            summed = summed + from_behind(owner_parts[REACH + offset], "dom", offset)
    remapped = (
        summed.reshape(owned, groups, levels, block_cells)
        .transpose(1, 2, 0, 3)
        .reshape(groups, levels, owned * block_cells)
    )
    members = groups * lax.axis_size("mem")
    norm_pairs = 2.0 * members * (members - 1)
    regrouped = lax.all_to_all(remapped, "mem", split_axis=2, concat_axis=0, tiled=True)
    part_cells = regrouped.shape[2]
    observed_part = lax.dynamic_slice_in_dim(
        observed, lax.axis_index("mem") * part_cells, part_cells, 1
    )
    skill_sum = jnp.sum(jnp.abs(regrouped - observed_part[None]), axis=0)
    spread = pair_total(regrouped, regrouped)
    score_part = skill_sum / members - spread / norm_pairs
    return lax.all_gather(score_part, "mem", axis=1, tiled=True)


def solution(mesh):
    return jax.shard_map(
        on_device,
        mesh=mesh,
        in_specs=(
            P("mem", None, "dom"),
            P(None, "dom"),
            P("dom", None, None),
            P("dom"),
            P("dom"),
            P("dom"),
        ),
        out_specs=P(None, "dom"),
        check_vma=False,
    )
```

profile of v0, /device:TPU:1, one launch (start us, length us, event | category | flops | bytes accessed | tf_op | source)
XLA Modules:
  0.0 215.5 jit_solution(2916523083471834512)
XLA Ops:
  0.0 0.8 compare_select_fusion
  0.8 0.8 compare_and_fusion
  1.6 1.7 copy.18
  3.4 1.8 copy.13
  5.9 4.8 %gather_fusion = bf16[96,192,128]{2,1,0:T(8,128)(2,1)} fusion(bf16[192,32,128]{2,0,1:T(8,128)(2,1)} %copy.13, s32[1024]{0:T(1024)S(1)} %pad_clamp_fusion), kind=kCustom, calls=%fused_computation | custom fusion | bytes 9437568 | tf_op jit(solution)/shard_map/jit(_take)/gather | solution.py:37
  10.7 3.4 %fusion.3 = f32[96,192,128]{2,1,0:T(8,128)S(1)} fusion(bf16[96,128,128]{2,1,0:T(8,128)(2,1)S(1)} %copy-done, bf16[96,192,128]{2,1,0:T(8,128)(2,1)} %gather_fusion, pred[96]{0:T(512)(128)(4,1)S(1)} %compare_and_fusion), kind=kOutput, calls=%fused_computation.6 | convolution fusion | flops 606339072 | bytes 17301600 | tf_op jit(solution)/shard_map/csi,sij->scj/dot_general | solution.py:38
  14.1 10.0 %fusion = f32[72,24576]{1,0:T(8,128)S(1)} fusion(f32[12,8,192,128]{3,2,1,0:T(8,128)S(1)} %bitcast.32, s32[96]{0:T(128)S(1)} %broadcast_subtract_fusion, pred[96]{0:T(512)(128)(4,1)S(1)} %iota_compare_fusion.1), kind=kOutput, calls=%fused_computation.3 | convolution fusion | flops 2038445568 | bytes 16515552 | tf_op jit(solution)/shard_map/dot_general | solution.py:48
  24.5 1.3 collective-permute-start
  25.8 1.3 collective-permute-start.1
  27.1 1.3 collective-permute-start.2
  28.4 1.9 collective-permute-start.3
  30.4 5.1 %collective-permute-start.4 = (f32[8,24576]{1,0:T(8,128)S(1)}, f32[8,24576]{1,0:T(8,128)S(1)}, u32[]{:S(2)}, u32[]{:S(2)}) collective-permute-start(f32[8,24576]{1,0:T(8,128)S(1)} %get-tuple-element.54), channel_id=1, source_target_pairs={{0,2},{2,4},{4,6},{6,8},{8,10},{10,12},{12,14},{14,16},{16,18},{18... | collective-permute-start | bytes 2359304 | tf_op jit(solution)/shard_map/ppermute | solution.py:13
  35.5 10.3 %collective-permute-done = f32[8,24576]{1,0:T(8,128)S(1)} collective-permute-done((f32[8,24576]{1,0:T(8,128)S(1)}, f32[8,24576]{1,0:T(8,128)S(1)}, u32[]{:S(2)}, u32[]{:S(2)}) %collective-permute-start) | collective-permute-done | bytes 786464 | tf_op jit(solution)/shard_map/ppermute | solution.py:13
  45.8 3.0 %collective-permute-start.5 = (f32[8,24576]{1,0:T(8,128)S(1)}, f32[8,24576]{1,0:T(8,128)S(1)}, u32[]{:S(2)}, u32[]{:S(2)}) collective-permute-start(f32[8,24576]{1,0:T(8,128)S(1)} %get-tuple-element.53), channel_id=1, source_target_pairs={{0,4},{2,6},{4,8},{6,10},{8,12},{10,14},{12,16},{14,18},{16,20},{1... | collective-permute-start | bytes 2359304 | tf_op jit(solution)/shard_map/ppermute | solution.py:13
  48.8 15.2 %collective-permute-done.1 = f32[8,24576]{1,0:T(8,128)S(1)} collective-permute-done((f32[8,24576]{1,0:T(8,128)S(1)}, f32[8,24576]{1,0:T(8,128)S(1)}, u32[]{:S(2)}, u32[]{:S(2)}) %collective-permute-start.1) | collective-permute-done | bytes 786464 | tf_op jit(solution)/shard_map/ppermute | solution.py:13
  64.1 12.9 %collective-permute-start.6 = (f32[8,24576]{1,0:T(8,128)S(1)}, f32[8,24576]{1,0:T(8,128)S(1)}, u32[]{:S(2)}, u32[]{:S(2)}) collective-permute-start(f32[8,24576]{1,0:T(8,128)S(1)} %get-tuple-element.52), channel_id=1, source_target_pairs={{0,6},{2,8},{4,10},{6,12},{8,14},{10,16},{12,18},{14,20},{16,22},{... | collective-permute-start | bytes 2359304 | tf_op jit(solution)/shard_map/ppermute | solution.py:13
  77.0 23.6 %collective-permute-start.7 = (f32[8,24576]{1,0:T(8,128)S(1)}, f32[8,24576]{1,0:T(8,128)S(1)}, u32[]{:S(2)}, u32[]{:S(2)}) collective-permute-start(f32[8,24576]{1,0:T(8,128)S(1)} %get-tuple-element.51), channel_id=1, source_target_pairs={{0,8},{2,10},{4,12},{6,14},{8,16},{10,18},{12,20},{14,22},{16,24},... | collective-permute-start | bytes 2359304 | tf_op jit(solution)/shard_map/ppermute | solution.py:13
  100.6 8.8 %collective-permute-done.7 = f32[8,24576]{1,0:T(8,128)S(1)} collective-permute-done((f32[8,24576]{1,0:T(8,128)S(1)}, f32[8,24576]{1,0:T(8,128)S(1)}, u32[]{:S(2)}, u32[]{:S(2)}) %collective-permute-start.7) | collective-permute-done | bytes 786464 | tf_op jit(solution)/shard_map/ppermute | solution.py:13
  109.5 1.2 fusion.14
  110.7 4.3 %copy.14 = f32[6,32,8,128]{1,0,3,2:T(8,128)} copy(f32[6,32,8,128]{3,2,1,0:T(8,128)} %bitcast.39) | data formatting | bytes 1572864 | tf_op jit(solution)/shard_map/transpose | solution.py:61
  114.9 4.0 %reshape.66 = f32[2,1,98304]{2,1,0:T(1,128)} reshape(f32[1024,6,32]{2,1,0:T(8,128)} %bitcast.33) | data formatting | bytes 1572864
  119.0 4.3 %all-to-all-start = ((f32[2,1,98304]{2,1,0:T(1,128)}), f32[2,1,98304]{2,1,0:T(1,128)}, u32[]{:S(2)}, u32[]{:S(2)}) async-start(f32[2,1,98304]{2,1,0:T(1,128)} %reshape.66), calls=%async_computation | async-start | bytes 1572864 | tf_op jit(solution)/shard_map/all_to_all | solution.py:66
  123.3 8.5 %all-to-all-done = f32[2,1,98304]{2,1,0:T(1,128)} async-done(((f32[2,1,98304]{2,1,0:T(1,128)}), f32[2,1,98304]{2,1,0:T(1,128)}, u32[]{:S(2)}, u32[]{:S(2)}) %all-to-all-start) | async-done | bytes 786464 | tf_op jit(solution)/shard_map/all_to_all | solution.py:66
  132.4 5.0 %reduce.1 = f32[2,98304]{1,0:T(2,128)} reduce(f32[2,1,98304]{2,1,0:T(1,128)} %all-to-all-done, f32[]{:T(128)} %broadcast.36), dimensions={1}, to_apply=%all_to_all.11.reduce_sub_computation | reduce | bytes 1572868 | tf_op jit(solution)/shard_map/all_to_all | solution.py:66
  137.4 4.7 %reshape.67 = f32[1024,6,32]{2,1,0:T(8,128)} reshape(f32[2,98304]{1,0:T(2,128)} %reduce.1) | data formatting | bytes 1572864
  142.1 4.4 %copy.17 = f32[6,32,2,512]{3,2,1,0:T(2,128)} copy(f32[6,32,2,512]{1,0,3,2:T(8,128)} %bitcast.34) | data formatting | bytes 1572864 | tf_op jit(solution)/shard_map/all_to_all | solution.py:66
  146.5 1.7 abs_reduce_fusion.1
  148.2 1.3 copy.16
  149.7 1.6 copy.20
  151.2 59.8 %while.11 = (s32[]{:T(128)}, f32[16,1024]{1,0:T(8,128)S(1)}, s32[16]{0:T(128)S(1)}, f32[12,16384]{1,0:T(8,128)}, s32[]{:T(128)}, /*index=5*/s32[]{:T(128)}, s32[]{:T(128)}) while((s32[]{:T(128)}, f32[16,1024]{1,0:T(8,128)S(1)}, s32[16]{0:T(128)S(1)}, f32[12,16384]{1,0:T(8,128)}, s32[]{:T(128)}, /*index=5*/s32[]{:T(128)}, s32[]{:T(128)}) %tuple.31), condition=%wide.region_3.4_spmd, body=%wide.region_1.3_spmd.sunk | while | flops 441349 | bytes 159875 | solution.py:28
  151.2 0.6 dynamic_slice.20
  153.8 1.0 constant_dynamic-slice_fusion.3
  155.0 0.6 dynamic_slice.20
  157.5 1.0 constant_dynamic-slice_fusion.3
  158.7 0.6 dynamic_slice.20
  161.2 1.0 constant_dynamic-slice_fusion.3
  162.5 0.6 dynamic_slice.20
  165.0 1.0 constant_dynamic-slice_fusion.3
  166.2 0.6 dynamic_slice.20
  168.7 1.0 constant_dynamic-slice_fusion.3
  169.9 0.6 dynamic_slice.20
  172.5 1.0 constant_dynamic-slice_fusion.3
  173.7 0.6 dynamic_slice.20
  176.2 1.0 constant_dynamic-slice_fusion.3
  177.4 0.6 dynamic_slice.20
  179.9 1.0 constant_dynamic-slice_fusion.3
  181.2 0.6 dynamic_slice.20
  183.7 1.0 constant_dynamic-slice_fusion.3
  184.9 0.6 dynamic_slice.20
  187.4 1.0 constant_dynamic-slice_fusion.3
  188.6 0.6 dynamic_slice.20
  191.2 1.0 constant_dynamic-slice_fusion.3
  192.4 0.6 dynamic_slice.20
  194.9 1.0 constant_dynamic-slice_fusion.3
  196.1 0.6 dynamic_slice.20
  198.6 1.0 constant_dynamic-slice_fusion.3
  199.9 0.6 dynamic_slice.20
  202.4 1.0 constant_dynamic-slice_fusion.3
  203.6 0.6 dynamic_slice.20
  206.1 1.0 constant_dynamic-slice_fusion.3
  207.3 0.6 dynamic_slice.20
  209.9 0.9 constant_dynamic-slice_fusion.3
  211.1 3.8 %all_gather.3 = f32[32,1024]{1,0:T(8,128)S(1)} all-gather(f32[32,512]{1,0:T(8,128)S(1)} %multiply_subtract_fusion), channel_id=1, replica_groups=mesh['dom'=16,'mem'=2] {'mem'}, dimensions={1}, use_global_device_ids=true | all-gather | bytes 196608 | tf_op jit(solution)/shard_map/all_gather | solution.py:74
  214.9 0.7 copy.34
  (55 shorter events, 4.8 us)
Async XLA Ops:
  0.0 10.7 %copy-start = (bf16[96,128,128]{2,1,0:T(8,128)(2,1)S(1)}, bf16[96,128,128]{2,1,0:T(8,128)(2,1)}, u32[]{:S(2)}) copy-start(bf16[96,128,128]{2,1,0:T(8,128)(2,1)} %param.10) | copy-start | bytes 9437188
  0.0 5.8 %copy-start.2 = (s32[96]{0:T(128)S(1)}, s32[96]{0:T(128)}, u32[]{:S(2)}) copy-start(s32[96]{0:T(128)} %param.12) | copy-start | bytes 1156
  24.5 21.3 %collective-permute-start = (f32[8,24576]{1,0:T(8,128)S(1)}, f32[8,24576]{1,0:T(8,128)S(1)}, u32[]{:S(2)}, u32[]{:S(2)}) collective-permute-start(f32[8,24576]{1,0:T(8,128)S(1)} %get-tuple-element.50), channel_id=1, source_target_pairs={{8,0},{10,2},{12,4},{14,6},{16,8},{18,10},{20,12},{22,14},{24,16},... | collective-permute-start | bytes 2359304 | tf_op jit(solution)/shard_map/ppermute | solution.py:13
  25.8 38.2 %collective-permute-start.1 = (f32[8,24576]{1,0:T(8,128)S(1)}, f32[8,24576]{1,0:T(8,128)S(1)}, u32[]{:S(2)}, u32[]{:S(2)}) collective-permute-start(f32[8,24576]{1,0:T(8,128)S(1)} %get-tuple-element.57), channel_id=1, source_target_pairs={{6,0},{8,2},{10,4},{12,6},{14,8},{16,10},{18,12},{20,14},{22,16},{... | collective-permute-start | bytes 2359304 | tf_op jit(solution)/shard_map/ppermute | solution.py:13
  27.1 49.9 %collective-permute-start.2 = (f32[8,24576]{1,0:T(8,128)S(1)}, f32[8,24576]{1,0:T(8,128)S(1)}, u32[]{:S(2)}, u32[]{:S(2)}) collective-permute-start(f32[8,24576]{1,0:T(8,128)S(1)} %get-tuple-element.56), channel_id=1, source_target_pairs={{4,0},{6,2},{8,4},{10,6},{12,8},{14,10},{16,12},{18,14},{20,16},{2... | collective-permute-start | bytes 2359304 | tf_op jit(solution)/shard_map/ppermute | solution.py:13
  28.4 72.2 %collective-permute-start.3 = (f32[8,24576]{1,0:T(8,128)S(1)}, f32[8,24576]{1,0:T(8,128)S(1)}, u32[]{:S(2)}, u32[]{:S(2)}) collective-permute-start(f32[8,24576]{1,0:T(8,128)S(1)} %get-tuple-element.55), channel_id=1, source_target_pairs={{2,0},{4,2},{6,4},{8,6},{10,8},{12,10},{14,12},{16,14},{18,16},{20... | collective-permute-start | bytes 2359304 | tf_op jit(solution)/shard_map/ppermute | solution.py:13
  30.4 70.2 %collective-permute-start.4 = (f32[8,24576]{1,0:T(8,128)S(1)}, f32[8,24576]{1,0:T(8,128)S(1)}, u32[]{:S(2)}, u32[]{:S(2)}) collective-permute-start(f32[8,24576]{1,0:T(8,128)S(1)} %get-tuple-element.54), channel_id=1, source_target_pairs={{0,2},{2,4},{4,6},{6,8},{8,10},{10,12},{12,14},{14,16},{16,18},{18... | collective-permute-start | bytes 2359304 | tf_op jit(solution)/shard_map/ppermute | solution.py:13
  45.8 54.8 %collective-permute-start.5 = (f32[8,24576]{1,0:T(8,128)S(1)}, f32[8,24576]{1,0:T(8,128)S(1)}, u32[]{:S(2)}, u32[]{:S(2)}) collective-permute-start(f32[8,24576]{1,0:T(8,128)S(1)} %get-tuple-element.53), channel_id=1, source_target_pairs={{0,4},{2,6},{4,8},{6,10},{8,12},{10,14},{12,16},{14,18},{16,20},{1... | collective-permute-start | bytes 2359304 | tf_op jit(solution)/shard_map/ppermute | solution.py:13
  64.1 36.6 %collective-permute-start.6 = (f32[8,24576]{1,0:T(8,128)S(1)}, f32[8,24576]{1,0:T(8,128)S(1)}, u32[]{:S(2)}, u32[]{:S(2)}) collective-permute-start(f32[8,24576]{1,0:T(8,128)S(1)} %get-tuple-element.52), channel_id=1, source_target_pairs={{0,6},{2,8},{4,10},{6,12},{8,14},{10,16},{12,18},{14,20},{16,22},{... | collective-permute-start | bytes 2359304 | tf_op jit(solution)/shard_map/ppermute | solution.py:13
  77.0 32.5 %collective-permute-start.7 = (f32[8,24576]{1,0:T(8,128)S(1)}, f32[8,24576]{1,0:T(8,128)S(1)}, u32[]{:S(2)}, u32[]{:S(2)}) collective-permute-start(f32[8,24576]{1,0:T(8,128)S(1)} %get-tuple-element.51), channel_id=1, source_target_pairs={{0,8},{2,10},{4,12},{6,14},{8,16},{10,18},{12,20},{14,22},{16,24},... | collective-permute-start | bytes 2359304 | tf_op jit(solution)/shard_map/ppermute | solution.py:13
  110.7 12.6 %copy-start.1 = (f32[32,1024]{1,0:T(8,128)S(1)}, f32[32,1024]{1,0:T(8,128)}, u32[]{:S(2)}) copy-start(f32[32,1024]{1,0:T(8,128)} %param.9) | copy-start | bytes 393220
  119.0 12.9 %all-to-all-start = ((f32[2,1,98304]{2,1,0:T(1,128)}), f32[2,1,98304]{2,1,0:T(1,128)}, u32[]{:S(2)}, u32[]{:S(2)}) async-start(f32[2,1,98304]{2,1,0:T(1,128)} %reshape.66), calls=%async_computation | async-start | bytes 1572864 | tf_op jit(solution)/shard_map/all_to_all | solution.py:66
where the time goes:
time: 217 us; the launch traced here: 216 us
  local copies, waits for them, and re-layouts  57.4 us (26%)
  starting transfers between devices  54.8 us (25%)
  waiting for transfers between devices  42.8 us (20%)
  loops' own time  31 us (14%)
  matrix products  13.4 us (6%)
  other arithmetic  11.4 us (5%)
  blocking collectives  3.78 us (2%)
    ppermute x8, starting transfers between devices, from_behind(): lax.ppermute(value, axis, [(source, source + steps) for source in range(f...  50.5 us
    ppermute x8, waiting for transfers between devices, from_behind(): lax.ppermute(value, axis, [(source, source + steps) for source in range(f...  34.4 us
    another operation x1, loops' own time, pair_total(): return lax.map(block_pairs, column_starts).reshape(left_set.shape[1:])  31 us
    dynamic_slice x16, local copies, waits for them, and re-layouts, block_pairs(): left_cols = lax.dynamic_slice_in_dim(flat_left, first_column, block_span, 1)  15.5 us
    unnamed x12, local copies, waits for them, and re-layouts  12.9 us
    dot_general x1, matrix products, on_device(): jnp.dot(chooser, partial_value.reshape(tile_slots, channels * block_cells...  10 us
    dynamic_slice x16, local copies, waits for them, and re-layouts, pair_total(): return lax.map(block_pairs, column_starts).reshape(left_set.shape[1:])  9.73 us
    all_to_all x1, waiting for transfers between devices, on_device(): lax.all_to_all(remapped, 'mem', split_axis=2, concat_axis=0, tiled=True)  8.48 us
  transfers between devices with their start and end apart: 9, of which 4 were waited for; matrix products, arithmetic and copies ran while one was open for 0% of the time, Pallas kernels for 0%

commit v1 on v0

--- a/solution.py
+++ b/solution.py
@@ -63,7 +63,9 @@
     )
     members = groups * lax.axis_size("mem")
     norm_pairs = 2.0 * members * (members - 1)
-    regrouped = lax.all_to_all(remapped, "mem", split_axis=2, concat_axis=0, tiled=True)
+    cells = jnp.split(remapped, lax.axis_size("mem"), axis=2)
+    received = lax.all_to_all(jnp.stack(cells), "mem", 0, 0)
+    regrouped = jnp.concatenate(received, axis=0)
     part_cells = regrouped.shape[2]
     observed_part = lax.dynamic_slice_in_dim(
         observed, lax.axis_index("mem") * part_cells, part_cells, 1

time: 217 us -> 199 us (0.917)
  local copies, waits for them, and re-layouts: 57.4 us -> 43.4 us
  other arithmetic: 11.4 us -> 6.89 us
    unnamed x12 -> x10, local copies, waits for them, and re-layouts: 12.9 us -> 5.25 us
    all_to_all x3 -> x0, local copies, waits for them, and re-layouts: 6.29 us -> none  [on_device(): lax.all_to_all(remapped, 'mem', split_axis=2, concat_axis=0, tiled=True)]
    all_to_all x1 -> x0, other arithmetic: 4.98 us -> none  [on_device(): lax.all_to_all(remapped, 'mem', split_axis=2, concat_axis=0, tiled=True)]
    transpose x1 -> x0, local copies, waits for them, and re-layouts: 4.26 us -> none  [on_device(): remapped = summed.reshape(owned, groups, levels, block_cells).transpose(1...]
    reshape x0 -> x1, local copies, waits for them, and re-layouts: none -> 2.21 us  [on_device(): remapped = summed.reshape(owned, groups, levels, block_cells).transpose(1...]
where the time goes in v1:
time: 199 us; the launch traced here: 197 us
  starting transfers between devices  54.8 us (28%)
  local copies, waits for them, and re-layouts  43.4 us (22%)
  waiting for transfers between devices  42.9 us (22%)
  loops' own time  31 us (16%)
  matrix products  13.4 us (7%)
  other arithmetic  6.89 us (3%)
  blocking collectives  3.78 us (2%)
    ppermute x8, starting transfers between devices, from_behind(): lax.ppermute(value, axis, [(source, source + steps) for source in range(f...  50.5 us
    ppermute x8, waiting for transfers between devices, from_behind(): lax.ppermute(value, axis, [(source, source + steps) for source in range(f...  34.4 us
    another operation x1, loops' own time, pair_total(): return lax.map(block_pairs, column_starts).reshape(left_set.shape[1:])  31 us
    dynamic_slice x16, local copies, waits for them, and re-layouts, block_pairs(): left_cols = lax.dynamic_slice_in_dim(flat_left, first_column, block_span, 1)  15.5 us
    dynamic_slice x16, local copies, waits for them, and re-layouts, pair_total(): return lax.map(block_pairs, column_starts).reshape(left_set.shape[1:])  10.4 us
    dot_general x1, matrix products, on_device(): jnp.dot(chooser, partial_value.reshape(tile_slots, channels * block_cells...  10 us
    all_to_all x1, waiting for transfers between devices, on_device(): received = lax.all_to_all(jnp.stack(cells), 'mem', 0, 0)  8.49 us
    unnamed x10, local copies, waits for them, and re-layouts  5.25 us
  transfers between devices with their start and end apart: 9, of which 4 were waited for; matrix products, arithmetic and copies ran while one was open for 0% of the time, Pallas kernels for 0%

profile of v1, /device:TPU:1, one launch (start us, length us, event | category | flops | bytes accessed | tf_op | source)
XLA Modules:
  0.0 197.0 jit_solution(6682831891145494302)
XLA Ops:
  0.0 0.8 compare_select_fusion
  0.8 0.8 compare_and_fusion
  1.6 1.7 copy.9
  3.4 1.8 copy.8
  5.9 4.9 %gather_fusion = bf16[96,192,128]{2,1,0:T(8,128)(2,1)} fusion(bf16[192,32,128]{2,0,1:T(8,128)(2,1)} %copy.8, s32[1024]{0:T(1024)S(1)} %pad_clamp_fusion), kind=kCustom, calls=%fused_computation | custom fusion | bytes 9437568 | tf_op jit(solution)/shard_map/jit(_take)/gather | solution.py:37
  10.7 3.4 %fusion.3 = f32[96,192,128]{2,1,0:T(8,128)S(1)} fusion(bf16[96,128,128]{2,1,0:T(8,128)(2,1)S(1)} %copy-done, bf16[96,192,128]{2,1,0:T(8,128)(2,1)} %gather_fusion, pred[96]{0:T(512)(128)(4,1)S(1)} %compare_and_fusion), kind=kOutput, calls=%fused_computation.6 | convolution fusion | flops 606339072 | bytes 17301600 | tf_op jit(solution)/shard_map/csi,sij->scj/dot_general | solution.py:38
  14.1 10.0 %fusion = f32[72,24576]{1,0:T(8,128)S(1)} fusion(f32[12,8,192,128]{3,2,1,0:T(8,128)S(1)} %bitcast.32, s32[96]{0:T(128)S(1)} %broadcast_subtract_fusion, pred[96]{0:T(512)(128)(4,1)S(1)} %iota_compare_fusion.1), kind=kOutput, calls=%fused_computation.3 | convolution fusion | flops 2038445568 | bytes 16515552 | tf_op jit(solution)/shard_map/dot_general | solution.py:48
  24.2 0.4 fusion.20
  24.6 1.3 collective-permute-start
  25.9 1.3 collective-permute-start.1
  27.2 1.3 collective-permute-start.2
  28.5 1.9 collective-permute-start.3
  30.4 5.1 %collective-permute-start.4 = (f32[8,24576]{1,0:T(8,128)S(1)}, f32[8,24576]{1,0:T(8,128)S(1)}, u32[]{:S(2)}, u32[]{:S(2)}) collective-permute-start(f32[8,24576]{1,0:T(8,128)S(1)} %get-tuple-element.54), channel_id=1, source_target_pairs={{0,2},{2,4},{4,6},{6,8},{8,10},{10,12},{12,14},{14,16},{16,18},{18... | collective-permute-start | bytes 2359304 | tf_op jit(solution)/shard_map/ppermute | solution.py:13
  35.5 10.3 %collective-permute-done = f32[8,24576]{1,0:T(8,128)S(1)} collective-permute-done((f32[8,24576]{1,0:T(8,128)S(1)}, f32[8,24576]{1,0:T(8,128)S(1)}, u32[]{:S(2)}, u32[]{:S(2)}) %collective-permute-start) | collective-permute-done | bytes 786464 | tf_op jit(solution)/shard_map/ppermute | solution.py:13
  45.8 3.0 %collective-permute-start.5 = (f32[8,24576]{1,0:T(8,128)S(1)}, f32[8,24576]{1,0:T(8,128)S(1)}, u32[]{:S(2)}, u32[]{:S(2)}) collective-permute-start(f32[8,24576]{1,0:T(8,128)S(1)} %get-tuple-element.53), channel_id=1, source_target_pairs={{0,4},{2,6},{4,8},{6,10},{8,12},{10,14},{12,16},{14,18},{16,20},{1... | collective-permute-start | bytes 2359304 | tf_op jit(solution)/shard_map/ppermute | solution.py:13
  48.9 15.2 %collective-permute-done.1 = f32[8,24576]{1,0:T(8,128)S(1)} collective-permute-done((f32[8,24576]{1,0:T(8,128)S(1)}, f32[8,24576]{1,0:T(8,128)S(1)}, u32[]{:S(2)}, u32[]{:S(2)}) %collective-permute-start.1) | collective-permute-done | bytes 786464 | tf_op jit(solution)/shard_map/ppermute | solution.py:13
  64.1 12.7 %collective-permute-start.6 = (f32[8,24576]{1,0:T(8,128)S(1)}, f32[8,24576]{1,0:T(8,128)S(1)}, u32[]{:S(2)}, u32[]{:S(2)}) collective-permute-start(f32[8,24576]{1,0:T(8,128)S(1)} %get-tuple-element.52), channel_id=1, source_target_pairs={{0,6},{2,8},{4,10},{6,12},{8,14},{10,16},{12,18},{14,20},{16,22},{... | collective-permute-start | bytes 2359304 | tf_op jit(solution)/shard_map/ppermute | solution.py:13
  76.9 23.8 %collective-permute-start.7 = (f32[8,24576]{1,0:T(8,128)S(1)}, f32[8,24576]{1,0:T(8,128)S(1)}, u32[]{:S(2)}, u32[]{:S(2)}) collective-permute-start(f32[8,24576]{1,0:T(8,128)S(1)} %get-tuple-element.51), channel_id=1, source_target_pairs={{0,8},{2,10},{4,12},{6,14},{8,16},{10,18},{12,20},{14,22},{16,24},... | collective-permute-start | bytes 2359304 | tf_op jit(solution)/shard_map/ppermute | solution.py:13
  100.7 8.8 %collective-permute-done.7 = f32[8,24576]{1,0:T(8,128)S(1)} collective-permute-done((f32[8,24576]{1,0:T(8,128)S(1)}, f32[8,24576]{1,0:T(8,128)S(1)}, u32[]{:S(2)}, u32[]{:S(2)}) %collective-permute-start.7) | collective-permute-done | bytes 786464 | tf_op jit(solution)/shard_map/ppermute | solution.py:13
  109.5 1.2 fusion.14
  110.7 2.2 %reshape.51 = f32[6,32,1024]{2,1,0:T(8,128)} reshape(f32[6,32,8,128]{3,2,1,0:T(8,128)} %bitcast.35) | data formatting | bytes 1572864 | tf_op jit(solution)/shard_map/reshape | solution.py:62
  112.9 1.2 slice_bitcast_fusion.1
  114.1 1.0 pad_maximum_fusion
  115.1 4.3 %all-to-all-start = ((f32[2,6,32,512]{3,2,1,0:T(8,128)}), f32[2,6,32,512]{3,2,1,0:T(8,128)}, u32[]{:S(2)}, u32[]{:S(2)}) async-start(f32[2,6,32,512]{3,2,1,0:T(8,128)} %pad_maximum_fusion), calls=%async_computation | async-start | bytes 1572864 | tf_op jit(solution)/shard_map/all_to_all | solution.py:67
  119.5 8.5 %all-to-all-done = f32[2,6,32,512]{3,2,1,0:T(8,128)} async-done(((f32[2,6,32,512]{3,2,1,0:T(8,128)}), f32[2,6,32,512]{3,2,1,0:T(8,128)}, u32[]{:S(2)}, u32[]{:S(2)}) %all-to-all-start) | async-done | bytes 786464 | tf_op jit(solution)/shard_map/all_to_all | solution.py:67
  127.9 1.2 pad.3
  129.2 1.6 copy.11
  130.8 60.5 %while.11 = (s32[]{:T(128)}, f32[16,1024]{1,0:T(8,128)S(1)}, s32[16]{0:T(128)S(1)}, f32[12,16384]{1,0:T(8,128)}, s32[]{:T(128)}, /*index=5*/s32[]{:T(128)}, s32[]{:T(128)}) while((s32[]{:T(128)}, f32[16,1024]{1,0:T(8,128)S(1)}, s32[16]{0:T(128)S(1)}, f32[12,16384]{1,0:T(8,128)}, s32[]{:T(128)}, /*index=5*/s32[]{:T(128)}, s32[]{:T(128)}) %tuple.32), condition=%wide.region_3.4_spmd, body=%wide.region_1.3_spmd.sunk | while | flops 441349 | bytes 159875 | solution.py:28
  130.8 0.6 dynamic_slice.20
  133.3 1.0 constant_dynamic-slice_fusion.3
  134.6 0.7 dynamic_slice.20
  137.1 1.0 constant_dynamic-slice_fusion.3
  138.4 0.7 dynamic_slice.20
  140.9 1.0 constant_dynamic-slice_fusion.3
  142.1 0.7 dynamic_slice.20
  144.7 1.0 constant_dynamic-slice_fusion.3
  145.9 0.7 dynamic_slice.20
  148.5 1.0 constant_dynamic-slice_fusion.3
  149.7 0.7 dynamic_slice.20
  152.3 1.0 constant_dynamic-slice_fusion.3
  153.2 0.1 abs_reduce_fusion.3
  153.5 0.7 dynamic_slice.20
  156.0 1.0 constant_dynamic-slice_fusion.3
  157.3 0.7 dynamic_slice.20
  159.8 1.0 constant_dynamic-slice_fusion.3
  161.1 0.7 dynamic_slice.20
  163.6 1.0 constant_dynamic-slice_fusion.3
  164.8 0.7 dynamic_slice.20
  167.4 1.0 constant_dynamic-slice_fusion.3
  168.6 0.7 dynamic_slice.20
  171.2 1.0 constant_dynamic-slice_fusion.3
  172.4 0.7 dynamic_slice.20
  175.0 1.0 constant_dynamic-slice_fusion.3
  176.2 0.7 dynamic_slice.20
  178.7 1.0 constant_dynamic-slice_fusion.3
  180.0 0.7 dynamic_slice.20
  182.5 1.0 constant_dynamic-slice_fusion.3
  183.7 0.7 dynamic_slice.20
  186.3 1.0 constant_dynamic-slice_fusion.3
  187.5 0.7 dynamic_slice.20
  190.1 0.9 constant_dynamic-slice_fusion.3
  191.3 1.2 abs_reduce_fusion.1
  192.6 3.8 %all_gather.3 = f32[32,1024]{1,0:T(8,128)S(1)} all-gather(f32[32,512]{1,0:T(8,128)S(1)} %multiply_subtract_fusion), channel_id=1, replica_groups=mesh['dom'=16,'mem'=2] {'mem'}, dimensions={1}, use_global_device_ids=true | all-gather | bytes 196608 | tf_op jit(solution)/shard_map/all_gather | solution.py:76
  196.3 0.7 copy.25
  (51 shorter events, 3.6 us)
Async XLA Ops:
  0.0 10.7 %copy-start = (bf16[96,128,128]{2,1,0:T(8,128)(2,1)S(1)}, bf16[96,128,128]{2,1,0:T(8,128)(2,1)}, u32[]{:S(2)}) copy-start(bf16[96,128,128]{2,1,0:T(8,128)(2,1)} %param.10) | copy-start | bytes 9437188
  0.0 5.8 %copy-start.2 = (s32[96]{0:T(128)S(1)}, s32[96]{0:T(128)}, u32[]{:S(2)}) copy-start(s32[96]{0:T(128)} %param.12) | copy-start | bytes 1156
  24.6 21.3 %collective-permute-start = (f32[8,24576]{1,0:T(8,128)S(1)}, f32[8,24576]{1,0:T(8,128)S(1)}, u32[]{:S(2)}, u32[]{:S(2)}) collective-permute-start(f32[8,24576]{1,0:T(8,128)S(1)} %get-tuple-element.50), channel_id=1, source_target_pairs={{8,0},{10,2},{12,4},{14,6},{16,8},{18,10},{20,12},{22,14},{24,16},... | collective-permute-start | bytes 2359304 | tf_op jit(solution)/shard_map/ppermute | solution.py:13
  25.9 38.2 %collective-permute-start.1 = (f32[8,24576]{1,0:T(8,128)S(1)}, f32[8,24576]{1,0:T(8,128)S(1)}, u32[]{:S(2)}, u32[]{:S(2)}) collective-permute-start(f32[8,24576]{1,0:T(8,128)S(1)} %get-tuple-element.57), channel_id=1, source_target_pairs={{6,0},{8,2},{10,4},{12,6},{14,8},{16,10},{18,12},{20,14},{22,16},{... | collective-permute-start | bytes 2359304 | tf_op jit(solution)/shard_map/ppermute | solution.py:13
  27.2 49.7 %collective-permute-start.2 = (f32[8,24576]{1,0:T(8,128)S(1)}, f32[8,24576]{1,0:T(8,128)S(1)}, u32[]{:S(2)}, u32[]{:S(2)}) collective-permute-start(f32[8,24576]{1,0:T(8,128)S(1)} %get-tuple-element.56), channel_id=1, source_target_pairs={{4,0},{6,2},{8,4},{10,6},{12,8},{14,10},{16,12},{18,14},{20,16},{2... | collective-permute-start | bytes 2359304 | tf_op jit(solution)/shard_map/ppermute | solution.py:13
  28.5 72.2 %collective-permute-start.3 = (f32[8,24576]{1,0:T(8,128)S(1)}, f32[8,24576]{1,0:T(8,128)S(1)}, u32[]{:S(2)}, u32[]{:S(2)}) collective-permute-start(f32[8,24576]{1,0:T(8,128)S(1)} %get-tuple-element.55), channel_id=1, source_target_pairs={{2,0},{4,2},{6,4},{8,6},{10,8},{12,10},{14,12},{16,14},{18,16},{20... | collective-permute-start | bytes 2359304 | tf_op jit(solution)/shard_map/ppermute | solution.py:13
  30.4 70.2 %collective-permute-start.4 = (f32[8,24576]{1,0:T(8,128)S(1)}, f32[8,24576]{1,0:T(8,128)S(1)}, u32[]{:S(2)}, u32[]{:S(2)}) collective-permute-start(f32[8,24576]{1,0:T(8,128)S(1)} %get-tuple-element.54), channel_id=1, source_target_pairs={{0,2},{2,4},{4,6},{6,8},{8,10},{10,12},{12,14},{14,16},{16,18},{18... | collective-permute-start | bytes 2359304 | tf_op jit(solution)/shard_map/ppermute | solution.py:13
  45.8 54.8 %collective-permute-start.5 = (f32[8,24576]{1,0:T(8,128)S(1)}, f32[8,24576]{1,0:T(8,128)S(1)}, u32[]{:S(2)}, u32[]{:S(2)}) collective-permute-start(f32[8,24576]{1,0:T(8,128)S(1)} %get-tuple-element.53), channel_id=1, source_target_pairs={{0,4},{2,6},{4,8},{6,10},{8,12},{10,14},{12,16},{14,18},{16,20},{1... | collective-permute-start | bytes 2359304 | tf_op jit(solution)/shard_map/ppermute | solution.py:13
  64.1 36.6 %collective-permute-start.6 = (f32[8,24576]{1,0:T(8,128)S(1)}, f32[8,24576]{1,0:T(8,128)S(1)}, u32[]{:S(2)}, u32[]{:S(2)}) collective-permute-start(f32[8,24576]{1,0:T(8,128)S(1)} %get-tuple-element.52), channel_id=1, source_target_pairs={{0,6},{2,8},{4,10},{6,12},{8,14},{10,16},{12,18},{14,20},{16,22},{... | collective-permute-start | bytes 2359304 | tf_op jit(solution)/shard_map/ppermute | solution.py:13
  76.9 32.6 %collective-permute-start.7 = (f32[8,24576]{1,0:T(8,128)S(1)}, f32[8,24576]{1,0:T(8,128)S(1)}, u32[]{:S(2)}, u32[]{:S(2)}) collective-permute-start(f32[8,24576]{1,0:T(8,128)S(1)} %get-tuple-element.51), channel_id=1, source_target_pairs={{0,8},{2,10},{4,12},{6,14},{8,16},{10,18},{12,20},{14,22},{16,24},... | collective-permute-start | bytes 2359304 | tf_op jit(solution)/shard_map/ppermute | solution.py:13
  110.7 8.7 %copy-start.1 = (f32[32,1024]{1,0:T(8,128)S(1)}, f32[32,1024]{1,0:T(8,128)}, u32[]{:S(2)}) copy-start(f32[32,1024]{1,0:T(8,128)} %param.9) | copy-start | bytes 393220
  115.1 12.9 %all-to-all-start = ((f32[2,6,32,512]{3,2,1,0:T(8,128)}), f32[2,6,32,512]{3,2,1,0:T(8,128)}, u32[]{:S(2)}, u32[]{:S(2)}) async-start(f32[2,6,32,512]{3,2,1,0:T(8,128)} %pad_maximum_fusion), calls=%async_computation | async-start | bytes 1572864 | tf_op jit(solution)/shard_map/all_to_all | solution.py:67
